TPU v7x, 32 devices: a whole 2x2x4 slice. The times are simulated.
32 devices in a mesh: replica: 2 (over y), sky: 4 (over z), freq: 4 (over x, core).
Axes of the slice: x: 2, y: 2, z: 4, core: 2. Of those that a mesh axis runs over, the one named last changes fastest.
Arguments:
- lightcone: bfloat16 [128, 32, 8, 128], P(('replica', 'freq'), None, 'sky'), parts along dimension 0, may hold values from -6 to 6
- cotangent: bfloat16 [128, 32, 8, 128], P(('replica', 'freq'), None, 'sky'), parts along dimension 0, may hold values from -6 to 6
- conv_weight: bfloat16 [32, 288], replicated, may hold values from -0.375 to 0.375
- in_proj: float32 [32, 16], replicated, may hold values from -1 to 1
- out_proj: float32 [32, 16], replicated, may hold values from -0.5 to 0.5
- skip_gain: float32 [32], replicated, may hold values from -4 to 4
- decay: float32 [64, 512], P('freq'), may hold values from 0.4 to 1
Outputs:
- d_lightcone: bfloat16 [128, 32, 8, 128], P(('replica', 'freq'), None, 'sky'), parts along dimension 0
- d_conv: float32 [64, 288], P('replica'), parts along dimension 0
- d_in_proj: float32 [64, 16], P('replica'), parts along dimension 0
- d_out_proj: float32 [64, 16], P('replica'), parts along dimension 0
- d_skip: float32 [64], P('replica'), parts along dimension 0
There are 2 independent parts, one for each index of `replica`. A program takes and returns all parts, laid end to end along the dimension named above; an argument that names none is the same for every part. Nothing has to cross between parts.
All inputs are finite; a program needn't handle non-finite values.
Results may differ from a plain program's by a relative error of at most 0.0055.
Values may be sent and summed in bfloat16 or wider, within the bound.
A program may use at most 128 MiB of HBM per device.

v0:
```python
import functools

import jax
import jax.numpy as jnp
from jax import lax
from jax.experimental import pallas as pl
from jax.experimental.pallas import tpu as pltpu
from jax.sharding import PartitionSpec as P

MESH = pl.DeviceIdType.MESH
BF = jnp.bfloat16
F32 = jnp.float32


def dot(a, b):
    return jnp.dot(a, b, preferred_element_type=F32)


def dot_nt(a, b):
    return lax.dot_general(a, b, (((1,), (1,)), ((), ())), preferred_element_type=F32)


def iota(shape, dim):
    return lax.broadcasted_iota(jnp.int32, shape, dim)


def kernel(nf, ns, x_ref, cot_ref, a_ref, b_ref, io_ref, skip_ref, dec_ref,
           dl_ref, pay_out,
           xr, cg, dg, inp, acc, p4, cur, k4, m4, kb, dr, tacc, pay, rs, sk, own,
           halo_s, halo_r, dhalo_s, dhalo_r, dec_s, dec_r, cot_s, cot_r, fwd_s,
           rs_s, rs_r, sk_s, sk_r, ag_s, ag_r):
    F = x_ref.shape[0]
    me = lax.axis_index("freq")
    sky = lax.axis_index("sky")
    core = lax.rem(me, 2)
    chip = me // 2
    chips = nf // 2
    sibling = me + 1 - 2 * core
    nxt = lax.rem(sky + 1, ns)
    prv = lax.rem(sky + ns - 1, ns)
    rows = pay.shape[0] // nf

    barrier = pltpu.get_barrier_semaphore()
    for d in range(1, nf):
        pl.semaphore_signal(barrier, inc=1, device_id={"freq": lax.rem(me + d, nf)}, device_id_type=MESH)
    for d in range(1, ns):
        pl.semaphore_signal(barrier, inc=1, device_id={"sky": lax.rem(sky + d, ns)}, device_id_type=MESH)

    pr, pc = iota((64, 64), 0), iota((64, 64), 1)
    perm = (pc == 2 * lax.rem(pr, 32) + pr // 32).astype(F32).astype(BF)
    for f in range(F):
        xr[f, 32:96, :] = dot(perm, x_ref[f]).astype(BF)
    for f in range(F):
        c2 = dot(perm, cot_ref[f]).astype(BF)
        cg[me, f * 32:(f + 1) * 32, 0:128] = c2[0:32]
        cg[me, f * 32:(f + 1) * 32, 128:256] = c2[32:64]
    dg[me] = dec_ref[...]
    pl.semaphore_wait(barrier, nf + ns - 2)

    def remote(src, dst, s, r, **where):
        return pltpu.make_async_remote_copy(
            src_ref=src, dst_ref=dst, send_sem=s, recv_sem=r, device_id=dict(where), device_id_type=MESH)

    def dec_copy(d):
        return remote(dg.at[me], dg.at[me], dec_s.at[d], dec_r.at[me], freq=jnp.maximum(me - d, 0))

    def cot_copy(d):
        target = jnp.maximum(chip - d, 0) * 2 + core
        return remote(cg.at[me], cg.at[me], cot_s.at[d], cot_r.at[me], freq=target)

    sib_copy = remote(cg.at[me], cg.at[me], cot_s.at[0], cot_r.at[me], freq=sibling)

    def fwd_copy(d):
        slot = jnp.minimum(chip + d, chips - 1) * 2 + core
        return remote(cg.at[slot], cg.at[slot], fwd_s.at[d], cot_r.at[slot], freq=sibling)

    up = remote(xr.at[:, 64:96], xr.at[:, 0:32], halo_s.at[0], halo_r.at[0], sky=nxt)
    down = remote(xr.at[:, 32:64], xr.at[:, 96:128], halo_s.at[1], halo_r.at[1], sky=prv)
    up.start()
    down.start()
    for d in range(1, nf):
        @pl.when(me >= d)
        def _():
            dec_copy(d).start()
    for d in range(1, chips):
        @pl.when(chip >= d)
        def _():
            cot_copy(d).start()

    @pl.when(core == 1)
    def _():
        sib_copy.start()

    sr, sc = iota((128, 256), 0), iota((128, 256), 1)
    shift = jnp.logical_or(lax.rem(sr + 1, 128) == sc, lax.rem(sr + 127, 128) == sc - 128)
    shift = shift.astype(F32).astype(BF)
    er = (iota((128, 2048), 1) // 16 == iota((128, 2048), 0)).astype(F32).astype(BF)
    et = (iota((2048, 128), 0) // 16 == iota((2048, 128), 1)).astype(F32).astype(BF)
    fi = iota((F, 512), 0)
    same = lax.rem(iota((32, 512), 1), 32) == iota((32, 512), 0)
    r64, l64 = iota((64, 128), 0), iota((64, 128), 1)
    diag = lax.rem(r64, 16) == 4 * (r64 // 16) + l64 // 32

    acc[...] = jnp.zeros_like(acc)
    tacc[...] = jnp.zeros_like(tacc)
    cur[...] = jnp.zeros_like(cur)

    up.wait_recv()
    down.wait_recv()
    for f in range(F):
        x = xr[f]
        rolled = dot(x, shift).astype(BF)
        full = jnp.concatenate([rolled[:, 0:128], x, rolled[:, 128:256]], axis=0)
        got = dot(a_ref[...], full).astype(BF)
        inp[f * 32:(f + 1) * 32, 0:128] = got[0:32]
        inp[f * 32:(f + 1) * 32, 128:256] = got[32:64]

    def block(d, carry):
        q = me + d

        @pl.when(d > 0)
        def _():
            pltpu.make_async_remote_copy(
                src_ref=dg.at[q], dst_ref=dg.at[q], send_sem=dec_s.at[0], recv_sem=dec_r.at[q],
                device_id={"freq": sibling}, device_id_type=MESH).wait_recv()

        v = cur[...]
        for g in range(F):
            v = jnp.where(fi == g - F * d, 1.0, v * dg[q, g:g + 1, :])
            G, j = g // 4, g % 4
            p4[G * 16:(G + 1) * 16, j * 512:(j + 1) * 512] = v
        cur[...] = v
        k = dot((p4[...] * io_ref[...]).astype(BF), et)
        k4[...] = k + jnp.where(jnp.logical_and(diag, d == 0), skip_ref[...], 0.0)
        for f in range(F):
            for G in range(4):
                row = jnp.broadcast_to(k4[G * 16 + f:G * 16 + f + 1, :], (32, 128))
                kb[f * 32:(f + 1) * 32, G * 128:(G + 1) * 128] = jnp.where(same[:, 0:128], row, 0.0).astype(BF)

        @pl.when(jnp.logical_and(d > 0, lax.rem(q, 2) == 0))
        def _():
            slot = q + core
            pltpu.make_async_remote_copy(
                src_ref=cg.at[slot], dst_ref=cg.at[slot], send_sem=fwd_s.at[0], recv_sem=cot_r.at[slot],
                device_id={"freq": sibling}, device_id_type=MESH).wait_recv()
            away = q // 2 - chip
            remote(cg.at[slot], cg.at[slot], fwd_s.at[away], cot_r.at[slot], freq=sibling).start()

        @pl.when(jnp.logical_and(d > 0, lax.rem(q, 2) != core))
        def _():
            pltpu.make_async_remote_copy(
                src_ref=cg.at[q], dst_ref=cg.at[q], send_sem=fwd_s.at[0], recv_sem=cot_r.at[q],
                device_id={"freq": sibling}, device_id_type=MESH).wait_recv()

        acc[...] += dot(kb[...], cg[q])
        gram = dot_nt(inp[...], cg[q])
        for f in range(F):
            row = jnp.sum(jnp.where(same, gram[f * 32:(f + 1) * 32, :], 0.0), axis=0, keepdims=True)
            for G in range(4):
                m4[G * 16 + f:G * 16 + f + 1, :] = row[:, G * 128:(G + 1) * 128]

        @pl.when(d == 0)
        def _():
            pay[96:128, :] = jnp.zeros((32, 128), F32)
            pay[100:101, :] = jnp.sum(jnp.where(diag, m4[...], 0.0), axis=0, keepdims=True)

        wide = dot(m4[...].astype(BF), er) * p4[...]
        tacc[...] += jnp.sum(wide.reshape(8, 8, 2048), axis=0)
        return carry

    lax.fori_loop(0, nf - me, block, 0)

    for f in range(F):
        dr[f, 32:64, :] = acc[f * 32:(f + 1) * 32, 0:128].astype(BF)
        dr[f, 64:96, :] = acc[f * 32:(f + 1) * 32, 128:256].astype(BF)
    dup = remote(dr.at[:, 64:96], dr.at[:, 0:32], dhalo_s.at[0], dhalo_r.at[0], sky=nxt)
    ddown = remote(dr.at[:, 32:64], dr.at[:, 96:128], dhalo_s.at[1], dhalo_r.at[1], sky=prv)
    dup.start()
    ddown.start()

    grad = jnp.zeros((192, 128), F32)
    for f in range(F):
        mid = dr[f, 32:96, :]
        rolled = dot(mid, shift).astype(BF)
        full = jnp.concatenate([rolled[:, 128:256], mid, rolled[:, 0:128]], axis=0)
        grad = grad + dot_nt(full, xr[f])
    for k in range(3):
        top = grad[k * 64:k * 64 + 32, 0:96]
        low = grad[k * 64 + 32:k * 64 + 64, 32:128]
        pay[k * 32:(k + 1) * 32, 0:96] = top + low
        pay[k * 32:(k + 1) * 32, 96:128] = jnp.zeros((32, 32), F32)
    t = jnp.sum(tacc[...], axis=0, keepdims=True)
    t = t[:, 0:512] + t[:, 512:1024] + t[:, 1024:1536] + t[:, 1536:2048]
    for k in range(4):
        pay[96 + k:97 + k, :] = t[:, k * 128:(k + 1) * 128]

    def part(ref, i):
        return ref.at[pl.ds(pl.multiple_of(i * rows, 8), rows)]

    def rs_copy(d):
        to = lax.rem(me + d, nf)
        return remote(part(pay, to), rs.at[d], rs_s.at[d], rs_r.at[d], freq=to)

    def sk_copy(d):
        return remote(own, sk.at[d], sk_s.at[d], sk_r.at[d], sky=lax.rem(sky + d, ns))

    def ag_copy(d):
        return remote(part(pay_out, me), part(pay_out, me), ag_s.at[d], ag_r.at[me],
                      freq=lax.rem(me + d, nf))

    def ag_wait(d):
        q = lax.rem(me + nf - d, nf)
        pltpu.make_async_remote_copy(
            src_ref=part(pay_out, q), dst_ref=part(pay_out, q), send_sem=ag_s.at[0], recv_sem=ag_r.at[q],
            device_id={"freq": q}, device_id_type=MESH).wait_recv()

    def light(f):
        x = dr[f]
        rolled = dot(x, shift).astype(BF)
        full = jnp.concatenate([rolled[:, 128:256], x, rolled[:, 0:128]], axis=0)
        dl_ref[f] = dot(b_ref[...], full).astype(BF)

    for d in range(1, nf):
        rs_copy(d).start()
    dup.wait_recv()
    ddown.wait_recv()
    for f in range(F // 2):
        light(f)
    total = pay[pl.ds(pl.multiple_of(me * rows, 8), rows), :]
    for d in range(1, nf):
        rs_copy(d).wait_recv()
        total = total + rs[d]
    own[...] = total
    for d in range(1, ns):
        sk_copy(d).start()
    for f in range(F // 2, F):
        light(f)
    for d in range(1, ns):
        sk_copy(d).wait_recv()
        total = total + sk[d]
    pay_out[pl.ds(pl.multiple_of(me * rows, 8), rows), :] = total
    for d in range(1, nf):
        ag_copy(d).start()
    for d in range(1, nf):
        ag_wait(d)

    up.wait_send()
    down.wait_send()
    dup.wait_send()
    ddown.wait_send()
    for d in range(1, nf):
        rs_copy(d).wait_send()
        ag_copy(d).wait_send()

        @pl.when(me >= d)
        def _():
            dec_copy(d).wait_send()
    for d in range(1, ns):
        sk_copy(d).wait_send()
    for d in range(1, chips):
        @pl.when(chip >= d)
        def _():
            cot_copy(d).wait_send()

        @pl.when(chip + d < chips)
        def _():
            fwd_copy(d).wait_send()

    @pl.when(core == 1)
    def _():
        sib_copy.wait_send()


def per_device(lightcone, cotangent, conv_weight, in_proj, out_proj, skip_gain, decay):
    F, C, R, W = lightcone.shape
    N = in_proj.shape[1]
    nf, ns = lax.axis_size("freq"), lax.axis_size("sky")
    scale = 1.0 / float(F * nf * R * ns * W) ** 0.5
    w4 = conv_weight.reshape(C, 3, 3, C)
    fw = w4.transpose(0, 2, 1, 3)
    bw = w4[:, ::-1].transpose(3, 2, 1, 0)

    def shifted(w, r):
        return jnp.pad(w, ((0, 0), (0, 0), (r, 1 - r), (0, 0))).reshape(C, 3 * 4 * C)

    a = jnp.concatenate([shifted(fw, 0), shifted(fw, 1)], axis=0)
    b = jnp.stack([shifted(bw, 0), shifted(bw, 1)], axis=1).reshape(2 * C, 3 * 4 * C)
    io = jnp.tile((in_proj * out_proj).reshape(1, C * N), (1, 4))
    skip4 = jnp.tile(skip_gain.reshape(1, C), (1, 4))
    rows = 128 // nf
    dma = pltpu.SemaphoreType.DMA
    vm = pl.BlockSpec(memory_space=pltpu.VMEM)
    dl, pay = pl.pallas_call(
        functools.partial(kernel, nf, ns),
        out_shape=(
            jax.ShapeDtypeStruct((F, C * R, W), BF),
            jax.ShapeDtypeStruct((128, 128), F32),
        ),
        in_specs=[vm] * 7,
        out_specs=(vm, vm),
        scratch_shapes=[
            pltpu.VMEM((F, 4 * C, W), BF),
            pltpu.VMEM((nf, F * C, R * W), BF),
            pltpu.VMEM((nf, F, C * N), F32),
            pltpu.VMEM((F * C, R * W), BF),
            pltpu.VMEM((F * C, R * W), F32),
            pltpu.VMEM((4 * F, 4 * C * N), F32),
            pltpu.VMEM((F, C * N), F32),
            pltpu.VMEM((4 * F, 128), F32),
            pltpu.VMEM((4 * F, 128), F32),
            pltpu.VMEM((F * C, F * C), BF),
            pltpu.VMEM((F, 4 * C, W), BF),
            pltpu.VMEM((8, 4 * C * N), F32),
            pltpu.VMEM((128, 128), F32),
            pltpu.VMEM((nf, rows, 128), F32),
            pltpu.VMEM((ns, rows, 128), F32),
            pltpu.VMEM((rows, 128), F32),
            dma((2,)), dma((2,)), dma((2,)), dma((2,)),
            dma((nf,)), dma((nf,)), dma((nf,)), dma((nf,)), dma((nf,)),
            dma((nf,)), dma((nf,)), dma((ns,)), dma((ns,)), dma((nf,)), dma((nf,)),
        ],
        compiler_params=pltpu.CompilerParams(
            collective_id=0, has_side_effects=True, vmem_limit_bytes=48 << 20),
    )(lightcone.reshape(F, C * R, W), cotangent.reshape(F, C * R, W), a, b, io, skip4, decay)
    grad = (pay[0:96, 0:96] * scale).reshape(3, C, 3, C).transpose(1, 2, 0, 3).reshape(C, 9 * C)
    t = (pay[96:100] * scale).reshape(C, N)
    d_skip = pay[100].reshape(4, C).sum(0) * scale
    return dl.reshape(F, C, R, W), grad, out_proj * t, in_proj * t, d_skip


def solution(mesh):
    return jax.shard_map(
        per_device,
        mesh=mesh,
        in_specs=(
            P(("replica", "freq"), None, "sky", None),
            P(("replica", "freq"), None, "sky", None),
            P(),
            P(),
            P(),
            P(),
            P("freq", None),
        ),
        out_specs=(
            P(("replica", "freq"), None, "sky", None),
            P("replica", None),
            P("replica", None),
            P("replica", None),
            P("replica"),
        ),
        check_vma=False,
    )
```

profile of v0, /device:TPU:0, one launch (start us, length us, event | category | flops | bytes accessed | tf_op | source)
XLA Modules:
  0.0 41.5 jit_solution(9730206245399318589)
XLA Ops:
  0.6 0.0 copy-start.3
  0.6 0.7 %tile.21 = f32[4,32]{1,0:T(4,128)S(1)} broadcast(f32[32]{0:T(128)} %param.12), dimensions={1} | broadcast | bytes 640 | tf_op jit(solution)/shard_map/tile | solution.py:289
  1.3 0.1 tile.22.skip_ref
  1.4 0.0 copy-done.3
  1.4 0.7 %mul.27 = f32[32,16]{0,1:T(8,128)S(1)} multiply(f32[32,16]{0,1:T(8,128)S(1)} %copy-done.3, f32[32,16]{0,1:T(8,128)} %param.11) | non-fusion elementwise | flops 512 | bytes 6144 | tf_op jit(solution)/shard_map/mul | solution.py:288
  2.1 0.1 copy.23
  2.2 0.1 tile.18
  2.3 0.0 copy-start.4
  2.3 0.0 copy-start.5
  2.3 0.1 copy.26
  2.4 0.6 %copy-done.4 = f32[32,16]{0,1:T(8,128)S(1)} copy-done((f32[32,16]{0,1:T(8,128)S(1)}, f32[32,16]{0,1:T(8,128)}, u32[]{:S(2)}) %copy-start.4) | copy-done | bytes 2072
  3.0 0.1 copy.25
  3.1 0.0 copy-done.5
  3.1 0.1 reshape.54
  3.3 0.1 copy.31
  3.4 0.2 fusion
  3.7 0.1 stack_reshape.6
  3.8 0.1 stack_reshape.7
  3.9 0.0 copy-start.2
  3.9 0.0 copy-start
  3.9 0.0 copy-start.1
  4.0 0.1 reshape.56
  4.2 0.1 reshape.55
  4.3 0.4 copy-done.2
  4.7 0.2 copy-done
  4.9 0.1 copy-done.1
  5.0 32.7 %shard_map.110 = (bf16[16,64,128]{2,1,0:T(8,128)(2,1)S(1)}, f32[128,128]{1,0:T(8,128)S(1)}) custom-call(bf16[16,64,128]{2,1,0:T(8,128)(2,1)S(1)} %bitcast.11, bf16[16,64,128]{2,1,0:T(8,128)(2,1)S(1)} %bitcast.12, bf16[64,384]{1,0:T(8,128)(2,1)S(1)} %pad_maximum_fusion.a_ref, bf16[64,384]{1,0:T(8,128)(2,1)S(1)} %reshape.57.b_ref, f32[1,2048]{1,0:T(1,128)S(1)} %bitcast.14, ...), custom_call_target="tpu_custom_call" | custom-call | tf_op jit(solution)/shard_map/pallas_call | solution.py:293
  37.7 0.1 reshape_squeeze.3
  37.9 0.5 %broadcast_multiply_fusion = f32[32]{0:T(128)} fusion(f32[32]{0:T(128)S(1)} %reduce_sum.9), kind=kLoop, calls=%fused_computation.7 | loop fusion | flops 32 | bytes 256 | tf_op jit(solution)/shard_map/mul | solution.py:327
  38.4 0.1 reshape.61
  38.5 0.7 %copy.28 = f32[32,16]{0,1:T(8,128)} copy(f32[32,16]{1,0:T(8,128)S(1)} %get-tuple-element.18) | data formatting | bytes 4096
  39.1 0.7 %copy.27 = f32[32,16]{0,1:T(8,128)} copy(f32[32,16]{1,0:T(8,128)S(1)} %get-tuple-element.19) | data formatting | bytes 4096
  39.8 0.1 reshape.59
  39.9 0.1 copy.24
  40.1 0.8 %reshape.60 = f32[32,288]{1,0:T(8,128)} reshape(f32[32,3,3,32]{3,2,1,0:T(4,128)S(1)} %copy.24) | data formatting | bytes 73728 | tf_op jit(solution)/shard_map/reshape | solution.py:325
  40.8 0.7 %copy.35 = bf16[16,32,2,128]{3,2,1,0:T(2,128)(2,1)} copy(bf16[16,32,2,128]{3,2,1,0:T(2,128)(2,1)S(1)} %bitcast.13) | data formatting | bytes 524288
  (13 shorter events, 0.2 us)
Async XLA Ops:
  0.6 0.8 %copy-start.3 = (f32[32,16]{0,1:T(8,128)S(1)}, f32[32,16]{0,1:T(8,128)}, u32[]{:S(2)}) copy-start(f32[32,16]{0,1:T(8,128)} %param.10) | copy-start | bytes 6148
  2.3 0.7 %copy-start.4 = (f32[32,16]{0,1:T(8,128)S(1)}, f32[32,16]{0,1:T(8,128)}, u32[]{:S(2)}) copy-start(f32[32,16]{0,1:T(8,128)} %param.11) | copy-start | bytes 6148
  2.3 0.8 %copy-start.5 = (bf16[32,288]{1,0:T(8,128)(2,1)S(1)}, bf16[32,288]{1,0:T(8,128)(2,1)}, u32[]{:S(2)}) copy-start(bf16[32,288]{1,0:T(8,128)(2,1)} %param.9) | copy-start | bytes 55300
  3.9 0.8 %copy-start.2 = (f32[16,512]{1,0:T(8,128)S(1)}, f32[16,512]{1,0:T(8,128)}, u32[]{:S(2)}) copy-start(f32[16,512]{1,0:T(8,128)} %dec_ref.1) | copy-start | bytes 98308
  3.9 1.0 %copy-start = (bf16[16,32,2,128]{3,2,1,0:T(2,128)(2,1)S(1)}, bf16[16,32,2,128]{3,2,1,0:T(2,128)(2,1)}, u32[]{:S(2)}) copy-start(bf16[16,32,2,128]{3,2,1,0:T(2,128)(2,1)} %param.7) | copy-start | bytes 786436
  3.9 1.0 %copy-start.1 = (bf16[16,32,2,128]{3,2,1,0:T(2,128)(2,1)S(1)}, bf16[16,32,2,128]{3,2,1,0:T(2,128)(2,1)}, u32[]{:S(2)}) copy-start(bf16[16,32,2,128]{3,2,1,0:T(2,128)(2,1)} %param.8) | copy-start | bytes 786436
where the time goes:
time: 41.8 us; the launch traced here: 41.5 us
  Pallas kernels  32.7 us (78%)
  local copies, waits for them, and re-layouts  6.7 us (16%)
  other arithmetic  1.28 us (3%)
  between operations  0.8 us (2%)
    pallas_call x1, Pallas kernels, per_device(): pl.pallas_call(functools.partial(kernel, nf, ns), out_shape=(jax.ShapeDty...  32.7 us
    unnamed x21, local copies, waits for them, and re-layouts  3.69 us
    reshape x2, local copies, waits for them, and re-layouts, per_device(): (pay[0:96, 0:96] * scale).reshape(3, C, 3, C).transpose(1, 2, 0, 3)  0.89 us

commit v1 on v0

v1 whole, which is shorter than its diff:
```python
import functools

import jax
import jax.numpy as jnp
from jax import lax
from jax.experimental import pallas as pl
from jax.experimental.pallas import tpu as pltpu
from jax.sharding import PartitionSpec as P

MESH = pl.DeviceIdType.MESH
BF = jnp.bfloat16
F32 = jnp.float32


def dot(a, b):
    return jnp.dot(a, b, preferred_element_type=F32)


def dot_nt(a, b):
    return lax.dot_general(a, b, (((1,), (1,)), ((), ())), preferred_element_type=F32)


def iota(shape, dim):
    return lax.broadcasted_iota(jnp.int32, shape, dim)


def kernel(nf, ns, x_ref, cot_ref, w_ref, in_ref, out_ref, skip_ref, dec_ref,
           dl_ref, pay_out,
           xr, cg, dg, inp, p4, cur, k4, m4, kb, dr, tacc, pay, rs, sk, own, aw, bw,
           halo_s, halo_r, dhalo_s, dhalo_r, dec_s, dec_r, cot_s, cot_r, fwd_s,
           rs_s, rs_r, sk_s, sk_r, ag_s, ag_r):
    F = x_ref.shape[0]
    me = lax.axis_index("freq")
    sky = lax.axis_index("sky")
    core = lax.rem(me, 2)
    chip = me // 2
    chips = nf // 2
    sibling = me + 1 - 2 * core
    nxt = lax.rem(sky + 1, ns)
    prv = lax.rem(sky + ns - 1, ns)
    rows = pay.shape[0] // nf

    barrier = pltpu.get_barrier_semaphore()
    for d in range(1, nf):
        pl.semaphore_signal(barrier, inc=1, device_id={"freq": lax.rem(me + d, nf)}, device_id_type=MESH)
    for d in range(1, ns):
        pl.semaphore_signal(barrier, inc=1, device_id={"sky": lax.rem(sky + d, ns)}, device_id_type=MESH)

    pr, pc = iota((64, 64), 0), iota((64, 64), 1)
    perm = (pc == 2 * lax.rem(pr, 32) + pr // 32).astype(F32).astype(BF)
    dg[me] = dec_ref[...]
    for f in range(F):
        c2 = dot(perm, cot_ref[f]).astype(BF)
        cg[me, 0, f * 32:(f + 1) * 32, :] = c2[0:32]
        cg[me, 1, f * 32:(f + 1) * 32, :] = c2[32:64]
    for f in range(F):
        xr[f, 32:96, :] = dot(perm, x_ref[f]).astype(BF)
    pl.semaphore_wait(barrier, nf + ns - 2)

    def remote(src, dst, s, r, **where):
        return pltpu.make_async_remote_copy(
            src_ref=src, dst_ref=dst, send_sem=s, recv_sem=r, device_id=dict(where), device_id_type=MESH)

    def dec_copy(d):
        return remote(dg.at[me], dg.at[me], dec_s.at[d], dec_r.at[me], freq=jnp.maximum(me - d, 0))

    def cot_copy(d, h):
        target = jnp.maximum(chip - d, 0) * 2 + core
        return remote(cg.at[me, h], cg.at[me, h], cot_s.at[d, h], cot_r.at[me, h], freq=target)

    def sib_copy(h):
        return remote(cg.at[me, h], cg.at[me, h], cot_s.at[0, h], cot_r.at[me, h], freq=sibling)

    def slot_copy(slot, h, s):
        return remote(cg.at[slot, h], cg.at[slot, h], s, cot_r.at[slot, h], freq=sibling)

    def fwd_copy(d, h):
        slot = jnp.minimum(chip + d, chips - 1) * 2 + core
        return slot_copy(slot, h, fwd_s.at[d, h])

    up = remote(xr.at[:, 64:96], xr.at[:, 0:32], halo_s.at[0], halo_r.at[0], sky=nxt)
    down = remote(xr.at[:, 32:64], xr.at[:, 96:128], halo_s.at[1], halo_r.at[1], sky=prv)
    for d in range(1, nf):
        @pl.when(me >= d)
        def _():
            dec_copy(d).start()
    for h in range(2):
        for d in range(1, chips):
            @pl.when(chip >= d)
            def _():
                cot_copy(d, h).start()

        @pl.when(core == 1)
        def _():
            sib_copy(h).start()
    up.start()
    down.start()

    sr, sc = iota((128, 256), 0), iota((128, 256), 1)
    shift = jnp.logical_or(lax.rem(sr + 1, 128) == sc, lax.rem(sr + 127, 128) == sc - 128)
    shift = shift.astype(F32).astype(BF)
    er = (iota((128, 2048), 1) // 16 == iota((128, 2048), 0)).astype(F32).astype(BF)
    et = (iota((2048, 128), 0) // 16 == iota((2048, 128), 1)).astype(F32).astype(BF)
    fi = iota((F, 512), 0)
    same = lax.rem(iota((32, 512), 1), 32) == iota((32, 512), 0)
    r64, l64 = iota((64, 128), 0), iota((64, 128), 1)
    diag = lax.rem(r64, 16) == 4 * (r64 // 16) + l64 // 32

    tacc[...] = jnp.zeros_like(tacc)
    cur[...] = jnp.zeros_like(cur)

    spread = (lax.rem(iota((32, 2048), 1) // 16, 32) == iota((32, 2048), 0)).astype(F32)
    io = jnp.dot(in_ref[...] * out_ref[...], spread, precision=lax.Precision.HIGHEST, preferred_element_type=F32)
    io = jnp.sum(jnp.where(lax.rem(iota((16, 2048), 1), 16) == iota((16, 2048), 0), io, 0.0), axis=0, keepdims=True)
    skip4 = jnp.concatenate([skip_ref[...]] * 4, axis=1)

    def factors(d, carry):
        q = me + d

        @pl.when(d > 0)
        def _():
            remote(dg.at[q], dg.at[q], dec_s.at[0], dec_r.at[q], freq=sibling).wait_recv()

        v = cur[...]
        for g in range(F):
            v = jnp.where(fi == g - F * d, 1.0, v * dg[q, g:g + 1, :])
            G, j = g // 4, g % 4
            p4[d, G * 16:(G + 1) * 16, j * 512:(j + 1) * 512] = v
        cur[...] = v
        k = dot((p4[d] * io).astype(BF), et)
        k4[...] = k + jnp.where(jnp.logical_and(diag, d == 0), skip4, 0.0)
        for f in range(F):
            for G in range(4):
                row = jnp.broadcast_to(k4[G * 16 + f:G * 16 + f + 1, :], (32, 128))
                kb[d, f * 32:(f + 1) * 32, G * 128:(G + 1) * 128] = jnp.where(same[:, 0:128], row, 0.0).astype(BF)
        return carry

    lax.fori_loop(0, nf - me, factors, 0)

    kk, ll = iota((288, 384), 0), iota((288, 384), 1)
    for r in range(2):
        tap = lax.rem(ll, 128) // 32 - r
        pick = jnp.logical_and(kk == (tap * 3 + ll // 128) * 32 + lax.rem(ll, 32),
                               jnp.logical_and(tap >= 0, tap <= 2))
        aw[r * 32:(r + 1) * 32, :] = dot(w_ref[...], pick.astype(F32).astype(BF)).astype(BF)
    mm, kk = iota((64, 288), 0), iota((64, 288), 1)
    for k in range(3):
        for row in range(4):
            tap = lax.rem(mm, 2) + 2 - row
            pick = jnp.logical_and(kk == (tap * 3 + k) * 32 + mm // 2,
                                   jnp.logical_and(tap >= 0, tap <= 2))
            at = k * 128 + row * 32
            bw[:, at:at + 32] = dot_nt(pick.astype(F32).astype(BF), w_ref[...])

    dup = remote(dr.at[:, 64:96], dr.at[:, 0:32], dhalo_s.at[1], dhalo_r.at[1], sky=nxt)
    ddown = remote(dr.at[:, 32:64], dr.at[:, 96:128], dhalo_s.at[0], dhalo_r.at[0], sky=prv)

    def mix(h):
        def step(d, total):
            q = me + d

            @pl.when(jnp.logical_and(d > 0, lax.rem(q, 2) == 0))
            def _():
                slot_copy(q + core, h, fwd_s.at[0, h]).wait_recv()
                slot_copy(q + core, h, fwd_s.at[q // 2 - chip, h]).start()

            @pl.when(jnp.logical_and(d > 0, lax.rem(q, 2) != core))
            def _():
                slot_copy(q, h, fwd_s.at[0, h]).wait_recv()

            return total + dot(kb[d], cg[q, h])

        total = lax.fori_loop(0, nf - me, step, jnp.zeros((F * 32, 128), F32)).astype(BF)
        for f in range(F):
            dr[f, 32 + 32 * h:64 + 32 * h, :] = total[f * 32:(f + 1) * 32]

    mix(0)
    ddown.start()
    up.wait_recv()
    down.wait_recv()
    for f in range(F):
        x = xr[f]
        rolled = dot(x, shift).astype(BF)
        full = jnp.concatenate([rolled[:, 0:128], x, rolled[:, 128:256]], axis=0)
        got = dot(aw[...], full).astype(BF)
        inp[f * 32:(f + 1) * 32, 0:128] = got[0:32]
        inp[f * 32:(f + 1) * 32, 128:256] = got[32:64]
    mix(1)
    dup.start()

    def block(d, carry):
        q = me + d
        gram = dot_nt(inp[...], jnp.concatenate([cg[q, 0], cg[q, 1]], axis=1))
        for f in range(F):
            row = jnp.sum(jnp.where(same, gram[f * 32:(f + 1) * 32, :], 0.0), axis=0, keepdims=True)
            for G in range(4):
                m4[G * 16 + f:G * 16 + f + 1, :] = row[:, G * 128:(G + 1) * 128]

        @pl.when(d == 0)
        def _():
            pay[96:128, :] = jnp.zeros((32, 128), F32)
            pay[100:101, :] = jnp.sum(jnp.where(diag, m4[...], 0.0), axis=0, keepdims=True)

        wide = dot(m4[...].astype(BF), er) * p4[d]
        tacc[...] += jnp.sum(wide.reshape(8, 8, 2048), axis=0)
        return carry

    lax.fori_loop(0, nf - me, block, 0)

    grad = jnp.zeros((192, 128), F32)
    for f in range(F):
        mid = dr[f, 32:96, :]
        rolled = dot(mid, shift).astype(BF)
        full = jnp.concatenate([rolled[:, 128:256], mid, rolled[:, 0:128]], axis=0)
        grad = grad + dot_nt(full, xr[f])
    for k in range(3):
        top = grad[k * 64:k * 64 + 32, 0:96]
        low = grad[k * 64 + 32:k * 64 + 64, 32:128]
        pay[k * 32:(k + 1) * 32, 0:96] = top + low
        pay[k * 32:(k + 1) * 32, 96:128] = jnp.zeros((32, 32), F32)
    t = jnp.sum(tacc[...], axis=0, keepdims=True)
    t = t[:, 0:512] + t[:, 512:1024] + t[:, 1024:1536] + t[:, 1536:2048]
    for k in range(4):
        pay[96 + k:97 + k, :] = t[:, k * 128:(k + 1) * 128]

    def part(ref, i):
        return ref.at[pl.ds(pl.multiple_of(i * rows, 8), rows)]

    def rs_copy(d):
        to = lax.rem(me + d, nf)
        return remote(part(pay, to), rs.at[d], rs_s.at[d], rs_r.at[d], freq=to)

    def sk_copy(d):
        return remote(own, sk.at[d], sk_s.at[d], sk_r.at[d], sky=lax.rem(sky + d, ns))

    def ag_copy(d):
        return remote(part(pay_out, me), part(pay_out, me), ag_s.at[d], ag_r.at[me],
                      freq=lax.rem(me + d, nf))

    def ag_wait(d):
        q = lax.rem(me + nf - d, nf)
        remote(part(pay_out, q), part(pay_out, q), ag_s.at[0], ag_r.at[q], freq=q).wait_recv()

    for d in range(1, nf):
        rs_copy(d).start()
    total = pay[pl.ds(pl.multiple_of(me * rows, 8), rows), :]
    for d in range(1, nf):
        rs_copy(d).wait_recv()
        total = total + rs[d]
    own[...] = total
    for d in range(1, ns):
        sk_copy(d).start()
    dup.wait_recv()
    ddown.wait_recv()
    b = bw[...].astype(BF)
    for f in range(F):
        x = dr[f]
        rolled = dot(x, shift).astype(BF)
        full = jnp.concatenate([rolled[:, 128:256], x, rolled[:, 0:128]], axis=0)
        dl_ref[f] = dot(b, full).astype(BF)
    for d in range(1, ns):
        sk_copy(d).wait_recv()
        total = total + sk[d]
    pay_out[pl.ds(pl.multiple_of(me * rows, 8), rows), :] = total
    for d in range(1, nf):
        ag_copy(d).start()
    for d in range(1, nf):
        ag_wait(d)

    up.wait_send()
    down.wait_send()
    dup.wait_send()
    ddown.wait_send()
    for d in range(1, nf):
        rs_copy(d).wait_send()
        ag_copy(d).wait_send()

        @pl.when(me >= d)
        def _():
            dec_copy(d).wait_send()
    for d in range(1, ns):
        sk_copy(d).wait_send()
    for h in range(2):
        for d in range(1, chips):
            @pl.when(chip >= d)
            def _():
                cot_copy(d, h).wait_send()

            @pl.when(chip + d < chips)
            def _():
                fwd_copy(d, h).wait_send()

        @pl.when(core == 1)
        def _():
            sib_copy(h).wait_send()


def finish(scale, dl_ref, pay_ref, in_ref, out_ref, dl_out, conv_out, din_out, dout_out, skip_out):
    dl_out[...] = dl_ref[...]
    for dr in range(3):
        for k in range(3):
            at = (dr * 3 + k) * 32
            conv_out[:, at:at + 32] = pay_ref[k * 32:(k + 1) * 32, dr * 32:(dr + 1) * 32] * scale
    t = jnp.concatenate([pay_ref[96 + k:97 + k, :] for k in range(4)], axis=1) * scale
    t = jnp.where(lax.rem(iota((16, 512), 1), 16) == iota((16, 512), 0), t, 0.0)
    join = (iota((512, 32), 0) // 16 == iota((512, 32), 1)).astype(F32)
    t = jnp.dot(t, join, precision=lax.Precision.HIGHEST, preferred_element_type=F32)
    din_out[...] = t * out_ref[...]
    dout_out[...] = t * in_ref[...]
    s = pay_ref[100:101, :] * scale
    skip_out[...] = s[:, 0:32] + s[:, 32:64] + s[:, 64:96] + s[:, 96:128]


def per_device(lightcone, cotangent, conv_weight, in_proj, out_proj, skip_gain, decay):
    F, C, R, W = lightcone.shape
    N = in_proj.shape[1]
    nf, ns = lax.axis_size("freq"), lax.axis_size("sky")
    scale = 1.0 / float(F * nf * R * ns * W) ** 0.5
    rows = 128 // nf
    dma = pltpu.SemaphoreType.DMA
    vm = pl.BlockSpec(memory_space=pltpu.VMEM)
    dl, pay = pl.pallas_call(
        functools.partial(kernel, nf, ns),
        out_shape=(
            jax.ShapeDtypeStruct((F, C * R, W), BF),
            jax.ShapeDtypeStruct((128, 128), F32),
        ),
        in_specs=[vm] * 7,
        out_specs=(vm, vm),
        scratch_shapes=[
            pltpu.VMEM((F, 4 * C, W), BF),
            pltpu.VMEM((nf, R, F * C, W), BF),
            pltpu.VMEM((nf, F, C * N), F32),
            pltpu.VMEM((F * C, R * W), BF),
            pltpu.VMEM((nf, 4 * F, 4 * C * N), F32),
            pltpu.VMEM((F, C * N), F32),
            pltpu.VMEM((4 * F, 128), F32),
            pltpu.VMEM((4 * F, 128), F32),
            pltpu.VMEM((nf, F * C, F * C), BF),
            pltpu.VMEM((F, 4 * C, W), BF),
            pltpu.VMEM((8, 4 * C * N), F32),
            pltpu.VMEM((128, 128), F32),
            pltpu.VMEM((nf, rows, 128), F32),
            pltpu.VMEM((ns, rows, 128), F32),
            pltpu.VMEM((rows, 128), F32),
            pltpu.VMEM((2 * C, 12 * C), BF),
            pltpu.VMEM((2 * C, 12 * C), F32),
            dma((2,)), dma((2,)), dma((2,)), dma((2,)),
            dma((nf,)), dma((nf,)), dma((nf, 2)), dma((nf, 2)), dma((nf, 2)),
            dma((nf,)), dma((nf,)), dma((ns,)), dma((ns,)), dma((nf,)), dma((nf,)),
        ],
        compiler_params=pltpu.CompilerParams(
            collective_id=0, has_side_effects=True, vmem_limit_bytes=48 << 20),
    )(lightcone.reshape(F, C * R, W), cotangent.reshape(F, C * R, W), conv_weight,
      in_proj.T, out_proj.T, skip_gain.reshape(1, C), decay)
    dl, grad, din, dout, d_skip = pl.pallas_call(
        functools.partial(finish, scale),
        out_shape=(
            jax.ShapeDtypeStruct((F, C * R, W), BF),
            jax.ShapeDtypeStruct((C, 9 * C), F32),
            jax.ShapeDtypeStruct((N, C), F32),
            jax.ShapeDtypeStruct((N, C), F32),
            jax.ShapeDtypeStruct((1, C), F32),
        ),
        in_specs=[vm] * 4,
        out_specs=(vm,) * 5,
        compiler_params=pltpu.CompilerParams(vmem_limit_bytes=4 << 20),
    )(dl, pay, in_proj.T, out_proj.T)
    return dl.reshape(F, C, R, W), grad, din.T, dout.T, d_skip.reshape(C)


def solution(mesh):
    return jax.shard_map(
        per_device,
        mesh=mesh,
        in_specs=(
            P(("replica", "freq"), None, "sky", None),
            P(("replica", "freq"), None, "sky", None),
            P(),
            P(),
            P(),
            P(),
            P("freq", None),
        ),
        out_specs=(
            P(("replica", "freq"), None, "sky", None),
            P("replica", None),
            P("replica", None),
            P("replica", None),
            P("replica"),
        ),
        check_vma=False,
    )
```

time: 41.8 us -> 35.3 us (0.84)
  Pallas kernels: 32.7 us -> 29.5 us
  local copies, waits for them, and re-layouts: 6.7 us -> 4.77 us
  other arithmetic: 1.28 us -> 0 us
    pallas_call x1, Pallas kernels: 32.7 us -> 28.5 us  [per_device(): pl.pallas_call(functools.partial(kernel, nf, ns), out_shape=(jax.ShapeDty...]
    reshape x7 -> x0, local copies, waits for them, and re-layouts: 1.34 us -> none  [the longest x2 0.89 us: per_device(): (pay[0:96, 0:96] * scale).reshape(3, C, 3, C).transpose(1, 2, 0, 3)]
    mul x5 -> x0, other arithmetic: 1.23 us -> none  [the longest x1 0.7 us: per_device(): io = jnp.tile((in_proj * out_proj).reshape(1, C * N), (1, 4))]
    another operation x7 -> x0, local copies, waits for them, and re-layouts: 1.19 us -> none  [the longest x2 0.75 us: per_device(): skip4 = jnp.tile(skip_gain.reshape(1, C), (1, 4))]
    unnamed x21 -> x14, local copies, waits for them, and re-layouts: 3.69 us -> 4.77 us
    pallas_call x0 -> x1, Pallas kernels: none -> 0.91 us  [per_device(): pl.pallas_call(functools.partial(finish, scale), out_shape=(jax.ShapeDtyp...]
where the time goes in v1:
time: 35.3 us; the launch traced here: 34.9 us
  Pallas kernels  29.5 us (84%)
  local copies, waits for them, and re-layouts  4.77 us (14%)
  between operations  0.66 us (2%)
    pallas_call x1, Pallas kernels, per_device(): pl.pallas_call(functools.partial(kernel, nf, ns), out_shape=(jax.ShapeDty...  28.5 us
    unnamed x14, local copies, waits for them, and re-layouts  4.77 us
    pallas_call x1, Pallas kernels, per_device(): pl.pallas_call(functools.partial(finish, scale), out_shape=(jax.ShapeDtyp...  0.91 us

profile of v1, /device:TPU:0, one launch (start us, length us, event | category | flops | bytes accessed | tf_op | source)
XLA Modules:
  0.0 34.9 jit_solution(4716443621453768294)
XLA Ops:
  0.6 0.0 copy-start.2
  0.6 0.0 copy-start.6
  0.7 0.7 %copy-done.2 = f32[32,16]{0,1:T(8,128)S(1)} copy-done((f32[32,16]{0,1:T(8,128)S(1)}, f32[32,16]{0,1:T(8,128)}, u32[]{:S(2)}) %copy-start.2) | copy-done | bytes 2072
  1.3 0.0 copy-done.6
  1.3 0.0 copy-start
  1.3 0.9 %copy-done = bf16[16,32,2,128]{3,2,1,0:T(2,128)(2,1)S(1)} copy-done((bf16[16,32,2,128]{3,2,1,0:T(2,128)(2,1)S(1)}, bf16[16,32,2,128]{3,2,1,0:T(2,128)(2,1)}, u32[]{:S(2)}) %copy-start) | copy-done | bytes 262168
  2.3 0.0 copy-start.1
  2.3 0.9 %copy-done.1 = bf16[16,32,2,128]{3,2,1,0:T(2,128)(2,1)S(1)} copy-done((bf16[16,32,2,128]{3,2,1,0:T(2,128)(2,1)S(1)}, bf16[16,32,2,128]{3,2,1,0:T(2,128)(2,1)}, u32[]{:S(2)}) %copy-start.1) | copy-done | bytes 262168
  3.2 0.0 copy-start.3
  3.2 0.7 %copy-done.3 = f32[32,16]{0,1:T(8,128)S(1)} copy-done((f32[32,16]{0,1:T(8,128)S(1)}, f32[32,16]{0,1:T(8,128)}, u32[]{:S(2)}) %copy-start.3) | copy-done | bytes 2072
  3.9 0.0 copy-start.4
  3.9 0.8 %copy-done.4 = f32[16,512]{1,0:T(8,128)S(1)} copy-done((f32[16,512]{1,0:T(8,128)S(1)}, f32[16,512]{1,0:T(8,128)}, u32[]{:S(2)}) %copy-start.4) | copy-done | bytes 32792
  4.7 0.0 copy-start.5
  4.7 0.7 %copy-done.5 = bf16[32,288]{1,0:T(8,128)(2,1)S(1)} copy-done((bf16[32,288]{1,0:T(8,128)(2,1)S(1)}, bf16[32,288]{1,0:T(8,128)(2,1)}, u32[]{:S(2)}) %copy-start.5) | copy-done | bytes 18456
  5.4 28.5 %shard_map.110 = (bf16[16,64,128]{2,1,0:T(8,128)(2,1)S(1)}, f32[128,128]{1,0:T(8,128)S(1)}) custom-call(bf16[16,64,128]{2,1,0:T(8,128)(2,1)S(1)} %bitcast.9, bf16[16,64,128]{2,1,0:T(8,128)(2,1)S(1)} %bitcast.10, bf16[32,288]{1,0:T(8,128)(2,1)S(1)} %copy-done.5, f32[16,32]{1,0:T(8,128)S(1)} %bitcast.11, f32[16,32]{1,0:T(8,128)S(1)} %bitcast.13, ...), custom_call_target="tpu_custom_call" | custom-call | tf_op jit(solution)/shard_map/pallas_call | solution.py:322
  34.0 0.9 %shard_map.111 = (bf16[16,64,128]{2,1,0:T(8,128)(2,1)}, f32[32,288]{1,0:T(8,128)}, f32[16,32]{1,0:T(8,128)}, f32[16,32]{1,0:T(8,128)}, f32[1,32]{1,0:T(1,128)}) custom-call(bf16[16,64,128]{2,1,0:T(8,128)(2,1)S(1)} %get-tuple-element.12.dl_ref, f32[128,128]{1,0:T(8,128)S(1)} %get-tuple-element.13.pay_ref, f32[16,32]{1,0:T(8,128)S(1)} %bitcast.12, ...), custom_call_target="tpu_custom_call" | custom-call | tf_op jit(solution)/shard_map/pallas_call | solution.py:356
Async XLA Ops:
  0.6 0.7 %copy-start.2 = (f32[32,16]{0,1:T(8,128)S(1)}, f32[32,16]{0,1:T(8,128)}, u32[]{:S(2)}) copy-start(f32[32,16]{0,1:T(8,128)} %param.10) | copy-start | bytes 6148
  0.6 0.7 %copy-start.6 = (f32[32]{0:T(128)S(1)}, f32[32]{0:T(128)}, u32[]{:S(2)}) copy-start(f32[32]{0:T(128)} %param.12) | copy-start | bytes 388
  1.3 1.0 %copy-start = (bf16[16,32,2,128]{3,2,1,0:T(2,128)(2,1)S(1)}, bf16[16,32,2,128]{3,2,1,0:T(2,128)(2,1)}, u32[]{:S(2)}) copy-start(bf16[16,32,2,128]{3,2,1,0:T(2,128)(2,1)} %param.7) | copy-start | bytes 786436
  2.3 0.9 %copy-start.1 = (bf16[16,32,2,128]{3,2,1,0:T(2,128)(2,1)S(1)}, bf16[16,32,2,128]{3,2,1,0:T(2,128)(2,1)}, u32[]{:S(2)}) copy-start(bf16[16,32,2,128]{3,2,1,0:T(2,128)(2,1)} %param.8) | copy-start | bytes 786436
  3.2 0.7 %copy-start.3 = (f32[32,16]{0,1:T(8,128)S(1)}, f32[32,16]{0,1:T(8,128)}, u32[]{:S(2)}) copy-start(f32[32,16]{0,1:T(8,128)} %param.11) | copy-start | bytes 6148
  3.9 0.8 %copy-start.4 = (f32[16,512]{1,0:T(8,128)S(1)}, f32[16,512]{1,0:T(8,128)}, u32[]{:S(2)}) copy-start(f32[16,512]{1,0:T(8,128)} %dec_ref.1) | copy-start | bytes 98308
  4.7 0.7 %copy-start.5 = (bf16[32,288]{1,0:T(8,128)(2,1)S(1)}, bf16[32,288]{1,0:T(8,128)(2,1)}, u32[]{:S(2)}) copy-start(bf16[32,288]{1,0:T(8,128)(2,1)} %w_ref.1) | copy-start | bytes 55300

commit v2 on v1

--- a/solution.py
+++ b/solution.py
@@ -24,11 +24,12 @@
     return lax.broadcasted_iota(jnp.int32, shape, dim)
 
 
-def kernel(nf, ns, x_ref, cot_ref, w_ref, in_ref, out_ref, skip_ref, dec_ref,
+def kernel(nf, ns, x_hbm, cot_hbm, w_hbm, in_hbm, out_hbm, skip_hbm, dec_hbm,
            dl_ref, pay_out,
            xr, cg, dg, inp, p4, cur, k4, m4, kb, dr, tacc, pay, rs, sk, own, aw, bw,
            halo_s, halo_r, dhalo_s, dhalo_r, dec_s, dec_r, cot_s, cot_r, fwd_s,
-           rs_s, rs_r, sk_s, sk_r, ag_s, ag_r):
+           rs_s, rs_r, sk_s, sk_r, ag_s, ag_r,
+           x_ref, cot_ref, w_ref, in_ref, out_ref, skip_ref, load):
     F = x_ref.shape[0]
     me = lax.axis_index("freq")
     sky = lax.axis_index("sky")
@@ -40,6 +41,14 @@
     prv = lax.rem(sky + ns - 1, ns)
     rows = pay.shape[0] // nf
 
+    loads = [
+        pltpu.make_async_copy(src, dst, load.at[i])
+        for i, (src, dst) in enumerate((
+            (cot_hbm, cot_ref), (dec_hbm, dg.at[me]), (x_hbm, x_ref), (w_hbm, w_ref),
+            (in_hbm, in_ref), (out_hbm, out_ref), (skip_hbm, skip_ref)))
+    ]
+    for one in loads:
+        one.start()
     barrier = pltpu.get_barrier_semaphore()
     for d in range(1, nf):
         pl.semaphore_signal(barrier, inc=1, device_id={"freq": lax.rem(me + d, nf)}, device_id_type=MESH)
@@ -48,13 +57,16 @@
 
     pr, pc = iota((64, 64), 0), iota((64, 64), 1)
     perm = (pc == 2 * lax.rem(pr, 32) + pr // 32).astype(F32).astype(BF)
-    dg[me] = dec_ref[...]
+    loads[0].wait()
     for f in range(F):
         c2 = dot(perm, cot_ref[f]).astype(BF)
         cg[me, 0, f * 32:(f + 1) * 32, :] = c2[0:32]
         cg[me, 1, f * 32:(f + 1) * 32, :] = c2[32:64]
+    loads[2].wait()
     for f in range(F):
         xr[f, 32:96, :] = dot(perm, x_ref[f]).astype(BF)
+    for i in (1, 3, 4, 5, 6):
+        loads[i].wait()
     pl.semaphore_wait(barrier, nf + ns - 2)
 
     def remote(src, dst, s, r, **where):
@@ -325,7 +337,7 @@
             jax.ShapeDtypeStruct((F, C * R, W), BF),
             jax.ShapeDtypeStruct((128, 128), F32),
         ),
-        in_specs=[vm] * 7,
+        in_specs=[pl.BlockSpec(memory_space=pltpu.MemorySpace.HBM)] * 7,
         out_specs=(vm, vm),
         scratch_shapes=[
             pltpu.VMEM((F, 4 * C, W), BF),
@@ -348,9 +360,16 @@
             dma((2,)), dma((2,)), dma((2,)), dma((2,)),
             dma((nf,)), dma((nf,)), dma((nf, 2)), dma((nf, 2)), dma((nf, 2)),
             dma((nf,)), dma((nf,)), dma((ns,)), dma((ns,)), dma((nf,)), dma((nf,)),
+            pltpu.VMEM((F, C * R, W), BF),
+            pltpu.VMEM((F, C * R, W), BF),
+            pltpu.VMEM((C, 9 * C), BF),
+            pltpu.VMEM((N, C), F32),
+            pltpu.VMEM((N, C), F32),
+            pltpu.VMEM((1, C), F32),
+            dma((7,)),
         ],
         compiler_params=pltpu.CompilerParams(
-            collective_id=0, has_side_effects=True, vmem_limit_bytes=48 << 20),
+            collective_id=0, has_side_effects=True, vmem_limit_bytes=63 << 20),
     )(lightcone.reshape(F, C * R, W), cotangent.reshape(F, C * R, W), conv_weight,
       in_proj.T, out_proj.T, skip_gain.reshape(1, C), decay)
     dl, grad, din, dout, d_skip = pl.pallas_call(
@@ -364,7 +383,7 @@
         ),
         in_specs=[vm] * 4,
         out_specs=(vm,) * 5,
-        compiler_params=pltpu.CompilerParams(vmem_limit_bytes=4 << 20),
+        compiler_params=pltpu.CompilerParams(vmem_limit_bytes=63 << 20),
     )(dl, pay, in_proj.T, out_proj.T)
     return dl.reshape(F, C, R, W), grad, din.T, dout.T, d_skip.reshape(C)
 

time: 35.3 us -> 32.4 us (0.918)
  local copies, waits for them, and re-layouts: 4.77 us -> 0 us
  Pallas kernels: 29.5 us -> 31.6 us
    unnamed x14 -> x0, local copies, waits for them, and re-layouts: 4.77 us -> none
    pallas_call x1, Pallas kernels: 28.5 us -> 29.7 us  [per_device(): pl.pallas_call(functools.partial(kernel, nf, ns), out_shape=(jax.ShapeDty...]
    pallas_call x1, Pallas kernels: 0.91 us -> 1.91 us  [per_device(): pl.pallas_call(functools.partial(finish, scale), out_shape=(jax.ShapeDtyp...]
where the time goes in v2:
time: 32.4 us; the launch traced here: 32.2 us
  Pallas kernels  31.6 us (98%)
  between operations  0.64 us (2%)
    pallas_call x1, Pallas kernels, per_device(): pl.pallas_call(functools.partial(kernel, nf, ns), out_shape=(jax.ShapeDty...  29.7 us
    pallas_call x1, Pallas kernels, per_device(): pl.pallas_call(functools.partial(finish, scale), out_shape=(jax.ShapeDtyp...  1.91 us

profile of v2, /device:TPU:0, one launch (start us, length us, event | category | flops | bytes accessed | tf_op | source)
XLA Modules:
  0.0 32.2 jit_solution(9908405305564223230)
XLA Ops:
  0.6 29.7 %shard_map.110 = (bf16[16,64,128]{2,1,0:T(8,128)(2,1)}, f32[128,128]{1,0:T(8,128)}) custom-call(bf16[16,64,128]{2,1,0:T(8,128)(2,1)} %bitcast.9, bf16[16,64,128]{2,1,0:T(8,128)(2,1)} %bitcast.10, bf16[32,288]{1,0:T(8,128)(2,1)} %w_hbm.1, f32[16,32]{1,0:T(8,128)} %bitcast.11, f32[16,32]{1,0:T(8,128)} %bitcast.13, f32[1,32]{1,0:T(1,128)} %bitcast.15, ...), custom_call_target="tpu_custom_call" | custom-call | tf_op jit(solution)/shard_map/pallas_call | solution.py:334
  30.3 1.9 %shard_map.111 = (bf16[16,64,128]{2,1,0:T(8,128)(2,1)}, f32[32,288]{1,0:T(8,128)}, f32[16,32]{1,0:T(8,128)}, f32[16,32]{1,0:T(8,128)}, f32[1,32]{1,0:T(1,128)}) custom-call(bf16[16,64,128]{2,1,0:T(8,128)(2,1)} %get-tuple-element.12.dl_ref, f32[128,128]{1,0:T(8,128)} %get-tuple-element.13.pay_ref, f32[16,32]{1,0:T(8,128)} %bitcast.12, f32[16,32]{1,0:T(8,128)} %bitcast.14), custom_call_target="tpu_custom_call" | custom-call | tf_op jit(solution)/shard_map/pallas_call | solution.py:375

commit v3 on v2

--- a/solution.py
+++ b/solution.py
@@ -255,6 +255,18 @@
 
     for d in range(1, nf):
         rs_copy(d).start()
+    dup.wait_recv()
+    ddown.wait_recv()
+    b = bw[...].astype(BF)
+
+    def light(f):
+        x = dr[f]
+        rolled = dot(x, shift).astype(BF)
+        full = jnp.concatenate([rolled[:, 128:256], x, rolled[:, 0:128]], axis=0)
+        dl_ref[f] = dot(b, full).astype(BF)
+
+    for f in range(F // 2):
+        light(f)
     total = pay[pl.ds(pl.multiple_of(me * rows, 8), rows), :]
     for d in range(1, nf):
         rs_copy(d).wait_recv()
@@ -262,14 +274,8 @@
     own[...] = total
     for d in range(1, ns):
         sk_copy(d).start()
-    dup.wait_recv()
-    ddown.wait_recv()
-    b = bw[...].astype(BF)
-    for f in range(F):
-        x = dr[f]
-        rolled = dot(x, shift).astype(BF)
-        full = jnp.concatenate([rolled[:, 128:256], x, rolled[:, 0:128]], axis=0)
-        dl_ref[f] = dot(b, full).astype(BF)
+    for f in range(F // 2, F):
+        light(f)
     for d in range(1, ns):
         sk_copy(d).wait_recv()
         total = total + sk[d]

time: 32.4 us -> 32.7 us (level)
  no operation moved by 1% of the time
where the time goes in v3:
time: 32.7 us; the launch traced here: 32.5 us
  Pallas kernels  31.9 us (98%)
  between operations  0.64 us (2%)
    pallas_call x1, Pallas kernels, per_device(): pl.pallas_call(functools.partial(kernel, nf, ns), out_shape=(jax.ShapeDty...  30 us
    pallas_call x1, Pallas kernels, per_device(): pl.pallas_call(functools.partial(finish, scale), out_shape=(jax.ShapeDtyp...  1.91 us

profile of v3, /device:TPU:0, one launch (start us, length us, event | category | flops | bytes accessed | tf_op | source)
XLA Modules:
  0.0 32.5 jit_solution(12187904183213030624)
XLA Ops:
  0.6 30.0 %shard_map.110 = (bf16[16,64,128]{2,1,0:T(8,128)(2,1)}, f32[128,128]{1,0:T(8,128)}) custom-call(bf16[16,64,128]{2,1,0:T(8,128)(2,1)} %bitcast.9, bf16[16,64,128]{2,1,0:T(8,128)(2,1)} %bitcast.10, bf16[32,288]{1,0:T(8,128)(2,1)} %w_hbm.1, f32[16,32]{1,0:T(8,128)} %bitcast.11, f32[16,32]{1,0:T(8,128)} %bitcast.13, f32[1,32]{1,0:T(1,128)} %bitcast.15, ...), custom_call_target="tpu_custom_call" | custom-call | tf_op jit(solution)/shard_map/pallas_call | solution.py:340
  30.6 1.9 %shard_map.111 = (bf16[16,64,128]{2,1,0:T(8,128)(2,1)}, f32[32,288]{1,0:T(8,128)}, f32[16,32]{1,0:T(8,128)}, f32[16,32]{1,0:T(8,128)}, f32[1,32]{1,0:T(1,128)}) custom-call(bf16[16,64,128]{2,1,0:T(8,128)(2,1)} %get-tuple-element.12.dl_ref, f32[128,128]{1,0:T(8,128)} %get-tuple-element.13.pay_ref, f32[16,32]{1,0:T(8,128)} %bitcast.12, f32[16,32]{1,0:T(8,128)} %bitcast.14), custom_call_target="tpu_custom_call" | custom-call | tf_op jit(solution)/shard_map/pallas_call | solution.py:381
